TPU v7x, 32 devices: a whole 2x2x4 slice. The times are simulated.
32 devices in a mesh: rep: 2 (over y), req: 4 (over z), mp: 4 (over x, core).
Axes of the slice: x: 2, y: 2, z: 4, core: 2. Of those that a mesh axis runs over, the one named last changes fastest.
Arguments:
- hidden_in: bfloat16 [128, 2, 8192], P(('rep', 'req'), None, 'mp'), parts along dimension 0, may hold values from -6 to 6
- frozen_query_rows: bfloat16 [128, 2, 8192], P(('rep', 'req'), None, 'mp'), parts along dimension 0, may hold values from -6 to 86
- new_kv: bfloat16 [128, 2, 2, 1024], P(('rep', 'req'), None, None, 'mp'), parts along dimension 0, may hold values from -6 to 31
- adapter_of: int32 [128], P(('rep', 'req')), parts along dimension 0, may hold values from 0 to 7, as said below
- adapter_home: int32 [16], P('rep'), parts along dimension 0, may hold values from 0 to 7, as said below
- a_store: bfloat16 [16, 64, 8192], P(('rep', 'req'), None, 'mp'), parts along dimension 0, may hold values from -0.0625 to 0.0625
- b_store: bfloat16 [16, 64, 8192], P(('rep', 'req'), None, 'mp'), parts along dimension 0, may hold values from -0.75 to 0.75
- kv_pool: bfloat16 [2, 1024, 16, 1024], P(None, ('rep', 'req'), None, 'mp'), parts along dimension 1, may hold values from -6 to 31
- page_table: int32 [128, 8], P(('rep', 'req')), parts along dimension 0, may hold values from 0 to 127, as said below
- cached_len: int32 [128], P(('rep', 'req')), parts along dimension 0, may hold values from 32 to 128
- new_group: int32 [128], P(('rep', 'req')), parts along dimension 0, may hold values from 0 to 3, as said below
Outputs:
- attended: bfloat16 [128, 2, 8192], P(('rep', 'req'), None, 'mp'), parts along dimension 0
- cache: bfloat16 [2, 128, 128, 1024], P(None, ('rep', 'req'), None, 'mp'), parts along dimension 1
There are 2 independent parts, one for each index of `rep`. A program takes and returns all parts, laid end to end along the dimension named above; each array names one. Nothing has to cross between parts.
Inputs may be any that keep to these rules, and one draw needn't show every extreme that they name: A permutation: adapter a lives in store slot adapter_home[a], which belongs to group adapter_home[a] div 2. `adapter_of`: the requests of one group (new rows h * 16 to h * 16 + 15) use adapters of min(16, number of groups) different owners, at most 4 requests an owner, a number reached in every group; all requests of one group whose adapters have one owner use the same adapter. `page_table`: the rows of one group name each of its 128 pages once. `new_group`: A request keeps its slot (row mod 16); the same 4 slots keep their group in every group; every group receives exactly one request into each slot; no group sends more than 3 requests to one other group, and some pair of groups reaches it.
All inputs are finite; a program needn't handle non-finite values.
Results may differ from a plain program's by a relative error of at most 0.0069.
Values may be sent and summed in bfloat16 or wider, within the bound.
A program may use at most 64 MiB of HBM per device.

v0:
```python
import jax
import jax.numpy as jnp
from jax import lax
from jax.sharding import PartitionSpec as P

HEAD = 128
NEG_FILL = -1e30


def attend(query_vectors, cached_keys, cached_values, length, fresh_kv):
    row_count, step_count, q_width = query_vectors.shape
    context = cached_keys.shape[1]
    kv_width = cached_keys.shape[2]
    kv_heads = kv_width // HEAD
    per_kv = q_width // kv_width
    score_scale = HEAD ** (-0.5)
    q_split = query_vectors.reshape(row_count, step_count, kv_heads, per_kv, HEAD)
    k_split = cached_keys.reshape(row_count, context, kv_heads, HEAD)
    v_split = cached_values.reshape(row_count, context, kv_heads, HEAD)
    new_keys = fresh_kv[:, :, 0].reshape(row_count, step_count, kv_heads, HEAD)
    new_values = fresh_kv[:, :, 1].reshape(row_count, step_count, kv_heads, HEAD)
    old_scores = (
        jnp.einsum("bskgd,bjkd->bskgj", q_split, k_split, preferred_element_type=jnp.float32)
        * score_scale
    )
    visible = jnp.arange(context)[None, :] < length[:, None]
    old_scores = jnp.where(visible[:, None, None, None, :], old_scores, NEG_FILL)
    new_scores = (
        jnp.einsum("bskgd,btkd->bskgt", q_split, new_keys, preferred_element_type=jnp.float32)
        * score_scale
    )
    causal = jnp.arange(step_count)[None, :] <= jnp.arange(step_count)[:, None]
    new_scores = jnp.where(causal[None, :, None, None, :], new_scores, NEG_FILL)
    scores = jnp.concatenate([old_scores, new_scores], axis=-1)
    row_max = jnp.max(scores, axis=-1, keepdims=True)
    weights = jnp.exp(scores - row_max)
    probabilities = (weights / jnp.sum(weights, axis=-1, keepdims=True)).astype(jnp.bfloat16)
    attention_out = jnp.einsum(
        "bskgj,bjkd->bskgd",
        probabilities[..., :context],
        v_split,
        preferred_element_type=jnp.float32,
    )
    attention_out = attention_out + jnp.einsum(
        "bskgt,btkd->bskgd",
        probabilities[..., context:],
        new_values,
        preferred_element_type=jnp.float32,
    )
    return attention_out.reshape(row_count, step_count, q_width).astype(jnp.bfloat16)


def adapter_rank_width(rank_partial_sum):
    return lax.psum(rank_partial_sum, "mp")


def per_device(
    hidden_in,
    frozen_query_rows,
    new_kv,
    adapter_of,
    adapter_home,
    a_store,
    b_store,
    kv_pool,
    page_table,
    cached_len,
    new_group,
):
    groups = lax.axis_size("req")
    my_group = lax.axis_index("req")
    per_group = adapter_of.shape[0]
    store_count = a_store.shape[0]
    context = page_table.shape[1] * kv_pool.shape[2]
    kv_width = kv_pool.shape[3]
    move_cap = -(-(per_group - per_group // 4) // groups)
    group_ids = jnp.arange(groups, dtype=jnp.int32)
    slot_ids = jnp.arange(per_group, dtype=jnp.int32)
    buffer_ids = jnp.arange(groups * move_cap, dtype=jnp.int32)
    adapter_slot = jnp.take(adapter_home, adapter_of)
    owners = adapter_slot // store_count
    local_pick = adapter_slot % store_count
    owner_hit = owners[:, None] == group_ids[None, :]
    wanted = jnp.max(jnp.where(owner_hit, local_pick[:, None], -1), axis=0)
    moving = new_group != my_group
    dest_hit = (new_group[:, None] == group_ids[None, :]) & moving[:, None]
    order_in = jnp.cumsum(dest_hit.astype(jnp.int32), axis=0) - 1
    position = jnp.sum(jnp.where(dest_hit, order_in, 0), axis=1)
    flat_slot = jnp.where(moving, new_group * move_cap + position, -1)
    slot_match = flat_slot[None, :] == buffer_ids[:, None]
    send_src = jnp.where(
        jnp.any(slot_match, axis=1),
        jnp.sum(jnp.where(slot_match, slot_ids[None, :], 0), axis=1),
        -1,
    )
    safe_src = jnp.maximum(send_src, 0)
    send_len = jnp.where(send_src >= 0, jnp.take(cached_len, safe_src), 0)
    got_wanted, got_slots, got_lens = (
        lax.all_to_all(wanted, "req", split_axis=0, concat_axis=0, tiled=True),
        lax.all_to_all(
            send_src.reshape(groups, move_cap), "req", split_axis=0, concat_axis=0, tiled=True
        ),
        lax.all_to_all(
            send_len.reshape(groups, move_cap), "req", split_axis=0, concat_axis=0, tiled=True
        ),
    )
    page_rows = jnp.take(kv_pool, page_table.reshape(-1), axis=1)
    cache_old = page_rows.reshape(2, per_group, context, kv_width)
    incoming = got_slots.reshape(-1)
    in_match = incoming[None, :] == slot_ids[:, None]
    in_index = jnp.sum(jnp.where(in_match, buffer_ids[None, :], 0), axis=1)
    len_new = jnp.where(moving, jnp.take(got_lens.reshape(-1), in_index), cached_len)
    wanted_slot = jnp.maximum(got_wanted, 0)
    a_panels, b_panels = (
        lax.all_to_all(
            jnp.take(a_store, wanted_slot, axis=0), "req", split_axis=0, concat_axis=0, tiled=True
        ),
        lax.all_to_all(
            jnp.take(b_store, wanted_slot, axis=0), "req", split_axis=0, concat_axis=0, tiled=True
        ),
    )
    a_rows = jnp.take(a_panels, owners, axis=0)
    up_panel_rows = jnp.take(b_panels, owners, axis=0)
    rank_slice_product = jnp.einsum(
        "rsd,rkd->rsk", hidden_in, a_rows, preferred_element_type=jnp.float32
    )
    complete_rank_product = adapter_rank_width(rank_slice_product).astype(jnp.bfloat16)
    adapter_query_delta = jnp.einsum(
        "gxj,gjv->gxv", complete_rank_product, up_panel_rows, preferred_element_type=jnp.float32
    )
    query_vectors = (frozen_query_rows.astype(jnp.float32) + adapter_query_delta).astype(
        jnp.bfloat16
    )
    far_cache = jnp.take(cache_old, safe_src, axis=1)
    send_pages = far_cache.reshape(2, groups, move_cap, context, kv_width)
    got_pages = lax.all_to_all(send_pages, "req", split_axis=1, concat_axis=1, tiled=True)
    pooled = jnp.concatenate(
        [cache_old, got_pages.reshape(2, groups * move_cap, context, kv_width)], axis=1
    )
    source = jnp.where(moving, per_group + in_index, slot_ids)
    cache_new = jnp.take(pooled, source, axis=1)
    attended = attend(query_vectors, cache_new[0], cache_new[1], len_new, new_kv)
    return (attended, cache_new)


def solution(mesh):
    placed = (
        P(("rep", "req"), None, "mp"),
        P(("rep", "req"), None, "mp"),
        P(("rep", "req"), None, None, "mp"),
        P(("rep", "req")),
        P("rep"),
        P(("rep", "req"), None, "mp"),
        P(("rep", "req"), None, "mp"),
        P(None, ("rep", "req"), None, "mp"),
        P(("rep", "req"), None),
        P(("rep", "req")),
        P(("rep", "req")),
    )
    return jax.shard_map(
        per_device,
        mesh=mesh,
        in_specs=placed,
        out_specs=(P(("rep", "req"), None, "mp"), P(None, ("rep", "req"), None, "mp")),
        check_vma=False,
    )
```

profile of v0, /device:TPU:0, one launch (start us, length us, event | category | flops | bytes accessed | tf_op | source)
XLA Modules:
  0.0 155.8 jit_solution(11224241576532435948)
XLA Ops:
  0.6 0.8 compare_select_fusion.3
  1.5 1.3 gather_fusion.5
  2.8 0.7 compare_and_fusion.1
  3.6 0.7 copy.112
  4.2 6.3 %all-to-all-start.3 = ((s32[4,1,1]{2,1,0:T(1,128)}), s32[4,1,1]{2,1,0:T(1,128)S(1)}, u32[]{:S(2)}, u32[]{:S(2)}) async-start(s32[4,1,1]{2,1,0:T(1,128)} %copy.112), calls=%async_computation.3 | async-start | bytes 4096 | tf_op jit(solution)/shard_map/all_to_all | solution.py:99
  10.5 0.7 broadcast_compare_fusion.1
  11.2 0.7 fusion.34
  12.0 0.8 select_reduce_fusion.3
  12.8 0.7 add_select_fusion
  13.5 0.1 fusion.32
  13.7 0.7 select_n.200
  14.4 1.3 gather_fusion.3
  15.8 1.3 select_select_fusion
  17.1 5.1 %all-to-all-start = ((s32[4,1,3]{2,1,0:T(1,128)}), s32[4,1,3]{2,1,0:T(1,128)S(1)}, u32[]{:S(2)}, u32[]{:S(2)}) async-start(s32[4,1,3]{2,1,0:T(1,128)} %bitcast), calls=%async_computation | async-start | bytes 4096 | tf_op jit(solution)/shard_map/all_to_all | solution.py:100
  22.2 0.2 maximum_reduce_fusion
  22.4 1.7 %gather_fusion.6 = bf16[4,64,2048]{2,1,0:T(8,128)(2,1)S(1)} fusion(bf16[2,64,2048]{2,1,0:T(8,128)(2,1)} %param.20, s32[1024]{0:T(1024)S(1)} %pad_clamp_fusion.1), kind=kCustom, calls=%fused_computation.clone | custom fusion | bytes 2097168 | tf_op jit(solution)/shard_map/jit(_take)/gather | solution.py:116
  24.0 2.6 %gather_fusion.8 = bf16[4,64,2048]{2,1,0:T(8,128)(2,1)} fusion(bf16[2,64,2048]{2,1,0:T(8,128)(2,1)} %param.21, s32[1024]{0:T(1024)S(1)} %pad_clamp_fusion.1), kind=kCustom, calls=%fused_computation.2.clone | custom fusion | bytes 2097168 | tf_op jit(solution)/shard_map/jit(_take)/gather | solution.py:119
  26.7 1.0 all-to-all-done
  27.6 4.1 %all-to-all-start.2 = ((s32[4,1,3]{2,1,0:T(1,128)}), s32[4,1,3]{2,1,0:T(1,128)S(1)}, u32[]{:S(2)}, u32[]{:S(2)}) async-start(s32[4,1,3]{2,1,0:T(1,128)} %bitcast.10), calls=%async_computation.2 | async-start | bytes 4096 | tf_op jit(solution)/shard_map/all_to_all | solution.py:103
  31.8 2.8 %broadcast_select_fusion.1 = (bf16[4,64,2048]{2,1,0:T(8,128)(2,1)}, bf16[4,64,2048]{2,1,0:T(8,128)(2,1)}) fusion(bf16[4,64,2048]{2,1,0:T(8,128)(2,1)S(1)} %gather_fusion.6, pred[4]{0:T(512)(128)(4,1)S(1)} %compare_and_fusion.2, bf16[4,64,2048]{2,1,0:T(8,128)(2,1)} %gather_fusion.8), kind=kLoop, calls=%fused_computation.36 | loop fusion | flops 1048576 | bytes 4194308 | tf_op jit(solution)/shard_map/jit(_take)/select_n | solution.py:116
  34.6 2.6 %all-to-all-done.2 = s32[4,1,3]{2,1,0:T(1,128)S(1)} async-done(((s32[4,1,3]{2,1,0:T(1,128)}), s32[4,1,3]{2,1,0:T(1,128)S(1)}, u32[]{:S(2)}, u32[]{:S(2)}) %all-to-all-start.2) | async-done | bytes 80 | tf_op jit(solution)/shard_map/all_to_all | solution.py:103
  37.1 3.5 %all-to-all-start.4 = ((bf16[4,64,2048]{2,1,0:T(8,128)(2,1)}), bf16[4,64,2048]{2,1,0:T(8,128)(2,1)S(1)}, u32[]{:S(2)}, u32[]{:S(2)}) async-start(bf16[4,64,2048]{2,1,0:T(8,128)(2,1)} %get-tuple-element.25), calls=%async_computation.4 | async-start | bytes 2097152 | tf_op jit(solution)/shard_map/all_to_all | solution.py:115
  40.8 23.4 %all-to-all-done.4 = bf16[4,64,2048]{2,1,0:T(8,128)(2,1)S(1)} async-done(((bf16[4,64,2048]{2,1,0:T(8,128)(2,1)}), bf16[4,64,2048]{2,1,0:T(8,128)(2,1)S(1)}, u32[]{:S(2)}, u32[]{:S(2)}) %all-to-all-start.4) | async-done | bytes 1048608 | tf_op jit(solution)/shard_map/all_to_all | solution.py:115
  64.2 4.2 %all-to-all-start.5 = ((bf16[4,64,2048]{2,1,0:T(8,128)(2,1)}), bf16[4,64,2048]{2,1,0:T(8,128)(2,1)}, u32[]{:S(2)}, u32[]{:S(2)}) async-start(bf16[4,64,2048]{2,1,0:T(8,128)(2,1)} %get-tuple-element.26), calls=%async_computation.5 | async-start | bytes 2097152 | tf_op jit(solution)/shard_map/all_to_all | solution.py:118
  68.5 2.0 %gather_fusion = bf16[128,2,16,256]{3,2,1,0:T(8,128)(2,1)} fusion(bf16[2,128,16,256]{3,2,1,0:T(8,128)(2,1)S(1)} %copy-done, s32[1024]{0:T(1024)S(1)} %pad_clamp_fusion.6), kind=kCustom, calls=%fused_computation.4 | custom fusion | bytes 4194816 | tf_op jit(solution)/shard_map/jit(_take)/gather | solution.py:107
  70.5 3.1 %copy.106 = bf16[2,128,16,256]{3,2,1,0:T(8,128)(2,1)} copy(bf16[2,128,16,256]{3,2,0,1:T(8,128)(2,1)} %bitcast.52) | data formatting | bytes 4194304 | tf_op jit(solution)/shard_map/jit(_take)/gather | solution.py:107
  73.9 2.8 %bitcast_select_fusion = bf16[2,16,128,256]{3,2,1,0:T(8,128)(2,1)} fusion(pred[16,128]{1,0:T(8,128)(4,1)S(1)} %broadcast_in_dim.159, bf16[2,16,128,256]{3,2,1,0:T(8,128)(2,1)} %bitcast.51), kind=kLoop, calls=%fused_computation.19 | loop fusion | flops 1048576 | bytes 4196352 | tf_op jit(solution)/shard_map/jit(_take)/select_n | solution.py:107
  76.7 3.4 %gather_fusion.1 = bf16[12,2,128,256]{3,2,1,0:T(8,128)(2,1)} fusion(bf16[2,16,128,256]{3,2,1,0:T(8,128)(2,1)} %bitcast_select_fusion, s32[1024]{0:T(1024)S(1)} %pad_clamp_fusion.5), kind=kCustom, calls=%fused_computation.5 | custom fusion | bytes 3145776 | tf_op jit(solution)/shard_map/jit(_take)/gather | solution.py:134
  80.2 0.2 slice_reduce_fusion
  80.4 0.6 reshape.370
  81.0 2.9 %copy_select_fusion = bf16[2,4,3,128,256]{4,3,2,0,1:T(8,128)(2,1)} fusion(bf16[2,4,3,128,256]{4,3,0,2,1:T(8,128)(2,1)} %bitcast.54, pred[4,3]{1,0:T(4,128)(4,1)S(1)} %le.81), kind=kLoop, calls=%fused_computation.23 | loop fusion | flops 786432 | bytes 3145740 | tf_op jit(solution)/shard_map/jit(_take)/select_n | solution.py:134
  83.9 9.9 %all-to-all-done.5 = bf16[4,64,2048]{2,1,0:T(8,128)(2,1)} async-done(((bf16[4,64,2048]{2,1,0:T(8,128)(2,1)}), bf16[4,64,2048]{2,1,0:T(8,128)(2,1)}, u32[]{:S(2)}, u32[]{:S(2)}) %all-to-all-start.5) | async-done | bytes 1048608 | tf_op jit(solution)/shard_map/all_to_all | solution.py:118
  93.8 4.3 %all-to-all-start.1 = ((bf16[2,4,3,128,256]{4,3,2,0,1:T(8,128)(2,1)}), bf16[2,4,3,128,256]{4,3,2,0,1:T(8,128)(2,1)}, u32[]{:S(2)}, u32[]{:S(2)}) async-start(bf16[2,4,3,128,256]{4,3,2,0,1:T(8,128)(2,1)} %copy_select_fusion), calls=%async_computation.1 | async-start | bytes 3145728 | tf_op jit(solution)/shard_map/all_to_all | solution.py:136
  98.1 0.6 iota_compare_fusion.5
  98.7 0.5 broadcast.414
  99.3 0.6 reduce.14
  100.0 0.6 reduce.15
  100.8 0.7 gather_fusion.4
  101.5 0.6 compare_and_fusion.3
  102.1 0.6 pad_clamp_fusion.4
  102.7 0.7 iota_compare_fusion.1
  103.3 2.8 %gather_fusion.7 = bf16[16,64,2048]{2,1,0:T(8,128)(2,1)} fusion(bf16[4,64,2048]{2,1,0:T(8,128)(2,1)S(1)} %all-to-all-done.4, s32[1024]{0:T(1024)S(1)} %pad_clamp_fusion), kind=kCustom, calls=%fused_computation.1.clone | custom fusion | bytes 8388672 | tf_op jit(solution)/shard_map/jit(_take)/gather | solution.py:122
  106.1 4.0 %gather_fusion.9 = bf16[16,64,2048]{2,1,0:T(8,128)(2,1)} fusion(bf16[4,64,2048]{2,1,0:T(8,128)(2,1)} %all-to-all-done.5, s32[1024]{0:T(1024)S(1)} %pad_clamp_fusion), kind=kCustom, calls=%fused_computation.3.clone | custom fusion | bytes 8388672 | tf_op jit(solution)/shard_map/jit(_take)/gather | solution.py:123
  110.1 3.5 %fusion.20 = f32[16,2,64]{2,1,0:T(2,128)S(1)} fusion(bf16[16,2,2048]{2,1,0:T(2,128)(2,1)S(1)} %copy-done.9, bf16[16,64,2048]{2,1,0:T(8,128)(2,1)} %gather_fusion.7, pred[16]{0:T(512)(128)(4,1)S(1)} %get-tuple-element.16), kind=kOutput, calls=%fused_computation.34 | convolution fusion | flops 10485760 | bytes 4333584 | tf_op jit(solution)/shard_map/rsd,rkd->rsk/dot_general | solution.py:124
  113.6 10.2 %psum.7 = bf16[16,2,64]{2,1,0:T(2,128)(2,1)S(1)} all-reduce(f32[16,2,64]{2,1,0:T(2,128)S(1)} %fusion.20), channel_id=1, replica_groups=mesh['rep'=2,'req'=4,'mp'=4] {'mp'}, use_global_device_ids=true, to_apply=%region_6.9 | all-reduce | flops 2048 | bytes 12288 | tf_op jit(solution)/shard_map/psum | solution.py:54
  123.8 2.9 %fusion.9 = bf16[16,2,2048]{2,1,0:T(2,128)(2,1)S(1)} fusion(bf16[16,64,2048]{2,1,0:T(8,128)(2,1)} %gather_fusion.9, pred[16]{0:T(512)(128)(4,1)S(1)} %get-tuple-element.16, bf16[16,2,2048]{2,1,0:T(2,128)(2,1)S(1)} %copy-done.10, bf16[16,2,64]{2,1,0:T(2,128)(2,1)S(1)} %psum.7), kind=kOutput, calls=%fused_computation.18 | convolution fusion | flops 10682368 | bytes 4460560 | tf_op jit(solution)/shard_map/gxj,gjv->gxv/dot_general | solution.py:128
  126.9 0.9 fusion.42
  127.8 6.8 %all-to-all-done.1 = bf16[2,4,3,128,256]{4,3,2,0,1:T(8,128)(2,1)} async-done(((bf16[2,4,3,128,256]{4,3,2,0,1:T(8,128)(2,1)}), bf16[2,4,3,128,256]{4,3,2,0,1:T(8,128)(2,1)}, u32[]{:S(2)}, u32[]{:S(2)}) %all-to-all-start.1) | async-done | bytes 1572896 | tf_op jit(solution)/shard_map/all_to_all | solution.py:136
  134.6 1.7 %copy.108 = bf16[2,4,3,128,256]{4,3,2,1,0:T(8,128)(2,1)S(1)} copy(bf16[2,4,3,128,256]{4,3,2,0,1:T(8,128)(2,1)} %all-to-all-done.1) | data formatting | bytes 3145728 | tf_op jit(solution)/shard_map/all_to_all | solution.py:136
  136.3 0.4 copy-done.2
  136.7 2.1 %pad_maximum_fusion = bf16[2,28,128,256]{3,2,1,0:T(8,128)(2,1)} fusion(bf16[2,12,128,256]{3,2,1,0:T(8,128)(2,1)S(1)} %bitcast.53, bf16[2,16,128,256]{3,2,1,0:T(8,128)(2,1)S(1)} %copy-done.2), kind=kLoop, calls=%fused_computation.16 | loop fusion | flops 1835008 | bytes 7340032 | tf_op jit(solution)/shard_map/concatenate | solution.py:137
  138.8 4.2 %gather_fusion.2 = bf16[16,2,128,256]{3,2,1,0:T(8,128)(2,1)} fusion(bf16[2,28,128,256]{3,2,1,0:T(8,128)(2,1)} %pad_maximum_fusion, s32[1024]{0:T(1024)} %pad_clamp_fusion.4), kind=kCustom, calls=%fused_computation.6 | custom fusion | bytes 4194368 | tf_op jit(solution)/shard_map/jit(_take)/gather | solution.py:141
  143.0 1.9 %select_bitcast_fusion = bf16[2,16,128,256]{3,2,0,1:T(8,128)(2,1)S(1)} fusion(bf16[16,2,128,256]{3,2,1,0:T(8,128)(2,1)} %gather_fusion.2, pred[16]{0:T(512)(128)(4,1)S(1)} %copy-done.8), kind=kLoop, calls=%fused_computation.22 | loop fusion | flops 1048576 | bytes 4194320 | tf_op jit(solution)/shard_map/jit(_take)/select_n | solution.py:141
  144.8 1.5 fusion.40
  146.3 1.5 copy.125
  147.8 1.6 %copy.111 = bf16[1,16,128,256]{2,3,1,0:T(8,128)(2,1)S(1)} copy(bf16[1,16,128,256]{3,2,0,1:T(8,128)(2,1)} %get-tuple-element.23) | data formatting | bytes 2097152 | tf_op jit(solution)/shard_map/slice | solution.py:142
  149.4 1.2 fusion.41
  150.6 0.8 reduce_max.32
  151.4 0.3 fusion.24
  151.7 0.9 divide_convert_fusion
  152.6 1.7 %copy.109 = bf16[1,16,128,256]{2,3,1,0:T(8,128)(2,1)S(1)} copy(bf16[1,16,128,256]{3,2,0,1:T(8,128)(2,1)} %get-tuple-element.24) | data formatting | bytes 2097152 | tf_op jit(solution)/shard_map/slice | solution.py:142
  154.3 0.6 convolution_bitcast_fusion.1
  154.9 0.2 fusion.19
  155.1 0.7 reshape.372
  (56 shorter events, 1.4 us)
Async XLA Ops:
  0.6 67.9 %copy-start = (bf16[2,128,16,256]{3,2,1,0:T(8,128)(2,1)S(1)}, bf16[2,128,16,256]{3,2,1,0:T(8,128)(2,1)}, u32[]{:S(2)}) copy-start(bf16[2,128,16,256]{3,2,1,0:T(8,128)(2,1)} %param.22) | copy-start | bytes 6291460
  4.2 12.9 %all-to-all-start.3 = ((s32[4,1,1]{2,1,0:T(1,128)}), s32[4,1,1]{2,1,0:T(1,128)S(1)}, u32[]{:S(2)}, u32[]{:S(2)}) async-start(s32[4,1,1]{2,1,0:T(1,128)} %copy.112), calls=%async_computation.3 | async-start | bytes 4096 | tf_op jit(solution)/shard_map/all_to_all | solution.py:99
  17.1 10.6 %all-to-all-start = ((s32[4,1,3]{2,1,0:T(1,128)}), s32[4,1,3]{2,1,0:T(1,128)S(1)}, u32[]{:S(2)}, u32[]{:S(2)}) async-start(s32[4,1,3]{2,1,0:T(1,128)} %bitcast), calls=%async_computation | async-start | bytes 4096 | tf_op jit(solution)/shard_map/all_to_all | solution.py:100
  27.6 9.5 %all-to-all-start.2 = ((s32[4,1,3]{2,1,0:T(1,128)}), s32[4,1,3]{2,1,0:T(1,128)S(1)}, u32[]{:S(2)}, u32[]{:S(2)}) async-start(s32[4,1,3]{2,1,0:T(1,128)} %bitcast.10), calls=%async_computation.2 | async-start | bytes 4096 | tf_op jit(solution)/shard_map/all_to_all | solution.py:103
  34.6 6.1 %copy-start.5 = (s32[16,8]{0,1:T(8,128)S(1)}, s32[16,8]{0,1:T(8,128)}, u32[]{:S(2)}) copy-start(s32[16,8]{0,1:T(8,128)} %param.23) | copy-start | bytes 1540
  37.1 27.1 %all-to-all-start.4 = ((bf16[4,64,2048]{2,1,0:T(8,128)(2,1)}), bf16[4,64,2048]{2,1,0:T(8,128)(2,1)S(1)}, u32[]{:S(2)}, u32[]{:S(2)}) async-start(bf16[4,64,2048]{2,1,0:T(8,128)(2,1)} %get-tuple-element.25), calls=%async_computation.4 | async-start | bytes 2097152 | tf_op jit(solution)/shard_map/all_to_all | solution.py:115
  64.2 29.5 %all-to-all-start.5 = ((bf16[4,64,2048]{2,1,0:T(8,128)(2,1)}), bf16[4,64,2048]{2,1,0:T(8,128)(2,1)}, u32[]{:S(2)}, u32[]{:S(2)}) async-start(bf16[4,64,2048]{2,1,0:T(8,128)(2,1)} %get-tuple-element.26), calls=%async_computation.5 | async-start | bytes 2097152 | tf_op jit(solution)/shard_map/all_to_all | solution.py:118
  76.7 3.5 %copy-start.4 = (bf16[16,2,2,256]{3,2,1,0:T(2,128)(2,1)S(1)}, bf16[16,2,2,256]{3,2,1,0:T(2,128)(2,1)}, u32[]{:S(2)}) copy-start(bf16[16,2,2,256]{3,2,1,0:T(2,128)(2,1)} %param.17) | copy-start | bytes 98308
  83.9 17.6 %copy-start.7 = (s32[16]{0:T(128)S(1)}, s32[16]{0:T(128)}, u32[]{:S(2)}) copy-start(s32[16]{0:T(128)} %param.25) | copy-start | bytes 196
  83.9 18.8 %copy-start.1 = (s32[16]{0:T(128)S(1)}, s32[16]{0:T(128)}, u32[]{:S(2)}) copy-start(s32[16]{0:T(128)} %param.24) | copy-start | bytes 196
  93.8 40.9 %all-to-all-start.1 = ((bf16[2,4,3,128,256]{4,3,2,0,1:T(8,128)(2,1)}), bf16[2,4,3,128,256]{4,3,2,0,1:T(8,128)(2,1)}, u32[]{:S(2)}, u32[]{:S(2)}) async-start(bf16[2,4,3,128,256]{4,3,2,0,1:T(8,128)(2,1)} %copy_select_fusion), calls=%async_computation.1 | async-start | bytes 3145728 | tf_op jit(solution)/shard_map/all_to_all | solution.py:136
  106.1 4.0 %copy-start.9 = (bf16[16,2,2048]{2,1,0:T(2,128)(2,1)S(1)}, bf16[16,2,2048]{2,1,0:T(2,128)(2,1)}, u32[]{:S(2)}) copy-start(bf16[16,2,2048]{2,1,0:T(2,128)(2,1)} %param.15) | copy-start | bytes 393220
  110.1 13.7 %copy-start.10 = (bf16[16,2,2048]{2,1,0:T(2,128)(2,1)S(1)}, bf16[16,2,2048]{2,1,0:T(2,128)(2,1)}, u32[]{:S(2)}) copy-start(bf16[16,2,2048]{2,1,0:T(2,128)(2,1)} %param.16) | copy-start | bytes 393220
  123.8 3.1 %copy-start.6 = (bf16[16,2,2,128]{3,2,1,0:T(2,128)(2,1)S(1)}, bf16[16,2,2,128]{3,2,1,0:T(2,128)(2,1)}, u32[]{:S(2)}) copy-start(bf16[16,2,2,128]{3,2,1,0:T(2,128)(2,1)} %reshape.370) | copy-start | bytes 49156
  123.8 3.1 %copy-start.11 = (pred[2,2]{1,0:T(4,128)(4,1)S(1)}, pred[2,2]{1,0:T(4,128)(4,1)}, u32[]{:S(2)}) copy-start(pred[2,2]{1,0:T(4,128)(4,1)} %iota_compare_fusion.5) | copy-start | bytes 16
  134.6 2.1 %copy-start.2 = (bf16[2,16,128,256]{3,2,1,0:T(8,128)(2,1)S(1)}, bf16[2,16,128,256]{3,2,1,0:T(8,128)(2,1)}, u32[]{:S(2)}) copy-start(bf16[2,16,128,256]{3,2,1,0:T(8,128)(2,1)} %bitcast_select_fusion) | copy-start | bytes 6291460
  138.8 4.2 %copy-start.8 = (pred[16]{0:T(512)(128)(4,1)S(1)}, pred[16]{0:T(512)(128)(4,1)}, u32[]{:S(2)}) copy-start(pred[16]{0:T(512)(128)(4,1)} %get-tuple-element.19) | copy-start | bytes 52
  152.6 1.7 %copy-start.3 = (bf16[16,2,2,8,130]{4,3,1,2,0:T(8,128)(2,1)S(1)}, bf16[16,2,2,8,130]{4,3,1,2,0:T(8,128)(2,1)}, u32[]{:S(2)}) copy-start(bf16[16,2,2,8,130]{4,3,1,2,0:T(8,128)(2,1)} %divide_convert_fusion) | copy-start | bytes 399364
where the time goes:
time: 157 us; the launch traced here: 156 us
  waiting for transfers between devices  43.7 us (28%)
  local copies, waits for them, and re-layouts  39.6 us (25%)
  starting transfers between devices  27.6 us (18%)
  other arithmetic  24.5 us (16%)
  blocking collectives  10.2 us (6%)
  matrix products  9.32 us (6%)
    all_to_all x1, waiting for transfers between devices, per_device(): lax.all_to_all(jnp.take(a_store, wanted_slot, axis=0), 'req', split_axis=...  23.4 us
    psum x1, blocking collectives, adapter_rank_width(): return lax.psum(rank_partial_sum, 'mp')  10.2 us
    all_to_all x1, waiting for transfers between devices, per_device(): lax.all_to_all(jnp.take(b_store, wanted_slot, axis=0), 'req', split_axis=...  9.87 us
    all_to_all x1, waiting for transfers between devices, per_device(): lax.all_to_all(send_pages, 'req', split_axis=1, concat_axis=1, tiled=True)  6.84 us
    all_to_all x1, starting transfers between devices, per_device(): lax.all_to_all(wanted, 'req', split_axis=0, concat_axis=0, tiled=True)  6.32 us
    gather x2, local copies, waits for them, and re-layouts, per_device(): page_rows = jnp.take(kv_pool, page_table.reshape(-1), axis=1)  5.1 us
    all_to_all x1, starting transfers between devices, per_device(): lax.all_to_all(send_src.reshape(groups, move_cap), 'req', split_axis=0, c...  5.09 us
    all_to_all x1, starting transfers between devices, per_device(): lax.all_to_all(send_pages, 'req', split_axis=1, concat_axis=1, tiled=True)  4.35 us
  transfers between devices with their start and end apart: 6, of which 5 were waited for; matrix products, arithmetic and copies ran while one was open for 31% of the time, Pallas kernels for 0%

commit v1 on v0

--- a/solution.py
+++ b/solution.py
@@ -51,7 +51,7 @@
 
 
 def adapter_rank_width(rank_partial_sum):
-    return lax.psum(rank_partial_sum, "mp")
+    return jnp.sum(lax.all_gather(rank_partial_sum, "mp"), axis=0)
 
 
 def per_device(

time: 157 us -> 157 us (level)
  waiting for transfers between devices: 43.7 us -> 49 us
  blocking collectives: 10.2 us -> 5.25 us
    psum x1 -> x0, blocking collectives: 10.2 us -> none  [adapter_rank_width(): return lax.psum(rank_partial_sum, 'mp')]
    all_gather x0 -> x1, blocking collectives: none -> 5.25 us  [adapter_rank_width(): return jnp.sum(lax.all_gather(rank_partial_sum, 'mp'), axis=0)]
    all_to_all x1, waiting for transfers between devices: 6.84 us -> 12.1 us  [per_device(): lax.all_to_all(send_pages, 'req', split_axis=1, concat_axis=1, tiled=True)]
where the time goes in v1:
time: 157 us; the launch traced here: 156 us
  waiting for transfers between devices  49 us (31%)
  local copies, waits for them, and re-layouts  39.5 us (25%)
  starting transfers between devices  27.6 us (18%)
  other arithmetic  24.3 us (15%)
  matrix products  9.27 us (6%)
  blocking collectives  5.25 us (3%)
    all_to_all x1, waiting for transfers between devices, per_device(): lax.all_to_all(jnp.take(a_store, wanted_slot, axis=0), 'req', split_axis=...  23.4 us
    all_to_all x1, waiting for transfers between devices, per_device(): lax.all_to_all(send_pages, 'req', split_axis=1, concat_axis=1, tiled=True)  12.1 us
    all_to_all x1, waiting for transfers between devices, per_device(): lax.all_to_all(jnp.take(b_store, wanted_slot, axis=0), 'req', split_axis=...  9.93 us
    all_to_all x1, starting transfers between devices, per_device(): lax.all_to_all(wanted, 'req', split_axis=0, concat_axis=0, tiled=True)  6.32 us
    all_gather x1, blocking collectives, adapter_rank_width(): return jnp.sum(lax.all_gather(rank_partial_sum, 'mp'), axis=0)  5.25 us
    gather x2, local copies, waits for them, and re-layouts, per_device(): page_rows = jnp.take(kv_pool, page_table.reshape(-1), axis=1)  5.1 us
    all_to_all x1, starting transfers between devices, per_device(): lax.all_to_all(send_src.reshape(groups, move_cap), 'req', split_axis=0, c...  5.09 us
    all_to_all x1, starting transfers between devices, per_device(): lax.all_to_all(send_pages, 'req', split_axis=1, concat_axis=1, tiled=True)  4.34 us
  transfers between devices with their start and end apart: 6, of which 5 were waited for; matrix products, arithmetic and copies ran while one was open for 31% of the time, Pallas kernels for 0%

profile of v1, /device:TPU:0, one launch (start us, length us, event | category | flops | bytes accessed | tf_op | source)
XLA Modules:
  0.0 155.8 jit_solution(5423815510068550758)
XLA Ops:
  0.6 0.8 compare_select_fusion.3
  1.5 1.3 gather_fusion.5
  2.8 0.7 compare_and_fusion.1
  3.6 0.7 copy.112
  4.2 6.3 %all-to-all-start.3 = ((s32[4,1,1]{2,1,0:T(1,128)}), s32[4,1,1]{2,1,0:T(1,128)S(1)}, u32[]{:S(2)}, u32[]{:S(2)}) async-start(s32[4,1,1]{2,1,0:T(1,128)} %copy.112), calls=%async_computation.3 | async-start | bytes 4096 | tf_op jit(solution)/shard_map/all_to_all | solution.py:99
  10.5 0.7 broadcast_compare_fusion.1
  11.2 0.7 fusion.34
  12.0 0.8 select_reduce_fusion.3
  12.8 0.7 add_select_fusion
  13.5 0.1 fusion.32
  13.7 0.7 select_n.200
  14.4 1.3 gather_fusion.3
  15.8 1.3 select_select_fusion
  17.1 5.1 %all-to-all-start = ((s32[4,1,3]{2,1,0:T(1,128)}), s32[4,1,3]{2,1,0:T(1,128)S(1)}, u32[]{:S(2)}, u32[]{:S(2)}) async-start(s32[4,1,3]{2,1,0:T(1,128)} %bitcast), calls=%async_computation | async-start | bytes 4096 | tf_op jit(solution)/shard_map/all_to_all | solution.py:100
  22.2 0.2 maximum_reduce_fusion
  22.4 1.7 %gather_fusion.6 = bf16[4,64,2048]{2,1,0:T(8,128)(2,1)S(1)} fusion(bf16[2,64,2048]{2,1,0:T(8,128)(2,1)} %param.20, s32[1024]{0:T(1024)S(1)} %pad_clamp_fusion.1), kind=kCustom, calls=%fused_computation.clone | custom fusion | bytes 2097168 | tf_op jit(solution)/shard_map/jit(_take)/gather | solution.py:116
  24.0 2.6 %gather_fusion.8 = bf16[4,64,2048]{2,1,0:T(8,128)(2,1)} fusion(bf16[2,64,2048]{2,1,0:T(8,128)(2,1)} %param.21, s32[1024]{0:T(1024)S(1)} %pad_clamp_fusion.1), kind=kCustom, calls=%fused_computation.2.clone | custom fusion | bytes 2097168 | tf_op jit(solution)/shard_map/jit(_take)/gather | solution.py:119
  26.7 1.0 all-to-all-done
  27.6 4.1 %all-to-all-start.2 = ((s32[4,1,3]{2,1,0:T(1,128)}), s32[4,1,3]{2,1,0:T(1,128)S(1)}, u32[]{:S(2)}, u32[]{:S(2)}) async-start(s32[4,1,3]{2,1,0:T(1,128)} %bitcast.10), calls=%async_computation.2 | async-start | bytes 4096 | tf_op jit(solution)/shard_map/all_to_all | solution.py:103
  31.8 2.8 %broadcast_select_fusion.1 = (bf16[4,64,2048]{2,1,0:T(8,128)(2,1)}, bf16[4,64,2048]{2,1,0:T(8,128)(2,1)}) fusion(bf16[4,64,2048]{2,1,0:T(8,128)(2,1)S(1)} %gather_fusion.6, pred[4]{0:T(512)(128)(4,1)S(1)} %compare_and_fusion.2, bf16[4,64,2048]{2,1,0:T(8,128)(2,1)} %gather_fusion.8), kind=kLoop, calls=%fused_computation.36 | loop fusion | flops 1048576 | bytes 4194308 | tf_op jit(solution)/shard_map/jit(_take)/select_n | solution.py:116
  34.6 2.6 %all-to-all-done.2 = s32[4,1,3]{2,1,0:T(1,128)S(1)} async-done(((s32[4,1,3]{2,1,0:T(1,128)}), s32[4,1,3]{2,1,0:T(1,128)S(1)}, u32[]{:S(2)}, u32[]{:S(2)}) %all-to-all-start.2) | async-done | bytes 80 | tf_op jit(solution)/shard_map/all_to_all | solution.py:103
  37.1 3.5 %all-to-all-start.4 = ((bf16[4,64,2048]{2,1,0:T(8,128)(2,1)}), bf16[4,64,2048]{2,1,0:T(8,128)(2,1)S(1)}, u32[]{:S(2)}, u32[]{:S(2)}) async-start(bf16[4,64,2048]{2,1,0:T(8,128)(2,1)} %get-tuple-element.25), calls=%async_computation.4 | async-start | bytes 2097152 | tf_op jit(solution)/shard_map/all_to_all | solution.py:115
  40.8 23.4 %all-to-all-done.4 = bf16[4,64,2048]{2,1,0:T(8,128)(2,1)S(1)} async-done(((bf16[4,64,2048]{2,1,0:T(8,128)(2,1)}), bf16[4,64,2048]{2,1,0:T(8,128)(2,1)S(1)}, u32[]{:S(2)}, u32[]{:S(2)}) %all-to-all-start.4) | async-done | bytes 1048608 | tf_op jit(solution)/shard_map/all_to_all | solution.py:115
  64.2 4.2 %all-to-all-start.5 = ((bf16[4,64,2048]{2,1,0:T(8,128)(2,1)}), bf16[4,64,2048]{2,1,0:T(8,128)(2,1)}, u32[]{:S(2)}, u32[]{:S(2)}) async-start(bf16[4,64,2048]{2,1,0:T(8,128)(2,1)} %get-tuple-element.26), calls=%async_computation.5 | async-start | bytes 2097152 | tf_op jit(solution)/shard_map/all_to_all | solution.py:118
  68.5 2.0 %gather_fusion = bf16[128,2,16,256]{3,2,1,0:T(8,128)(2,1)} fusion(bf16[2,128,16,256]{3,2,1,0:T(8,128)(2,1)S(1)} %copy-done, s32[1024]{0:T(1024)S(1)} %pad_clamp_fusion.6), kind=kCustom, calls=%fused_computation.4 | custom fusion | bytes 4194816 | tf_op jit(solution)/shard_map/jit(_take)/gather | solution.py:107
  70.5 3.1 %copy.106 = bf16[2,128,16,256]{3,2,1,0:T(8,128)(2,1)} copy(bf16[2,128,16,256]{3,2,0,1:T(8,128)(2,1)} %bitcast.53) | data formatting | bytes 4194304 | tf_op jit(solution)/shard_map/jit(_take)/gather | solution.py:107
  73.9 2.8 %bitcast_select_fusion = bf16[2,16,128,256]{3,2,1,0:T(8,128)(2,1)} fusion(pred[16,128]{1,0:T(8,128)(4,1)S(1)} %broadcast_in_dim.159, bf16[2,16,128,256]{3,2,1,0:T(8,128)(2,1)} %bitcast.52), kind=kLoop, calls=%fused_computation.19 | loop fusion | flops 1048576 | bytes 4196352 | tf_op jit(solution)/shard_map/jit(_take)/select_n | solution.py:107
  76.7 3.4 %gather_fusion.1 = bf16[12,2,128,256]{3,2,1,0:T(8,128)(2,1)} fusion(bf16[2,16,128,256]{3,2,1,0:T(8,128)(2,1)} %bitcast_select_fusion, s32[1024]{0:T(1024)S(1)} %pad_clamp_fusion.5), kind=kCustom, calls=%fused_computation.5 | custom fusion | bytes 3145776 | tf_op jit(solution)/shard_map/jit(_take)/gather | solution.py:134
  80.2 0.2 slice_reduce_fusion
  80.4 0.6 reshape.371
  81.0 2.8 %copy_select_fusion = bf16[2,4,3,128,256]{4,3,2,0,1:T(8,128)(2,1)} fusion(bf16[2,4,3,128,256]{4,3,0,2,1:T(8,128)(2,1)} %bitcast.55, pred[4,3]{1,0:T(4,128)(4,1)S(1)} %le.81), kind=kLoop, calls=%fused_computation.23 | loop fusion | flops 786432 | bytes 3145740 | tf_op jit(solution)/shard_map/jit(_take)/select_n | solution.py:134
  83.8 9.9 %all-to-all-done.5 = bf16[4,64,2048]{2,1,0:T(8,128)(2,1)} async-done(((bf16[4,64,2048]{2,1,0:T(8,128)(2,1)}), bf16[4,64,2048]{2,1,0:T(8,128)(2,1)}, u32[]{:S(2)}, u32[]{:S(2)}) %all-to-all-start.5) | async-done | bytes 1048608 | tf_op jit(solution)/shard_map/all_to_all | solution.py:118
  93.8 4.3 %all-to-all-start.1 = ((bf16[2,4,3,128,256]{4,3,2,0,1:T(8,128)(2,1)}), bf16[2,4,3,128,256]{4,3,2,0,1:T(8,128)(2,1)}, u32[]{:S(2)}, u32[]{:S(2)}) async-start(bf16[2,4,3,128,256]{4,3,2,0,1:T(8,128)(2,1)} %copy_select_fusion), calls=%async_computation.1 | async-start | bytes 3145728 | tf_op jit(solution)/shard_map/all_to_all | solution.py:136
  98.1 0.5 iota_compare_fusion.5
  98.7 0.5 broadcast.414
  99.1 0.6 reduce.14
  99.8 0.6 reduce.15
  100.6 0.7 gather_fusion.4
  101.3 0.5 compare_and_fusion.3
  101.8 0.6 pad_clamp_fusion.4
  102.4 0.7 iota_compare_fusion.1
  103.1 2.7 %gather_fusion.7 = bf16[16,64,2048]{2,1,0:T(8,128)(2,1)} fusion(bf16[4,64,2048]{2,1,0:T(8,128)(2,1)S(1)} %all-to-all-done.4, s32[1024]{0:T(1024)S(1)} %pad_clamp_fusion), kind=kCustom, calls=%fused_computation.1.clone | custom fusion | bytes 8388672 | tf_op jit(solution)/shard_map/jit(_take)/gather | solution.py:122
  105.8 3.4 %fusion.20 = f32[16,2,64]{2,1,0:T(2,128)S(1)} fusion(bf16[16,2,2048]{2,1,0:T(2,128)(2,1)S(1)} %copy-done.9, bf16[16,64,2048]{2,1,0:T(8,128)(2,1)} %gather_fusion.7, pred[16]{0:T(512)(128)(4,1)S(1)} %get-tuple-element.16), kind=kOutput, calls=%fused_computation.34 | convolution fusion | flops 10485760 | bytes 4333584 | tf_op jit(solution)/shard_map/rsd,rkd->rsk/dot_general | solution.py:124
  109.3 5.2 %all-gather = f32[64,2,64]{2,1,0:T(2,128)S(1)} all-gather(f32[16,2,64]{2,1,0:T(2,128)S(1)} %fusion.20), channel_id=2, replica_groups=mesh['rep'=2,'req'=4,'mp'=4] {'mp'}, dimensions={0}, use_global_device_ids=true | all-gather | bytes 40960 | tf_op jit(solution)/shard_map/all_gather | solution.py:54
  114.6 4.0 %gather_fusion.9 = bf16[16,64,2048]{2,1,0:T(8,128)(2,1)} fusion(bf16[4,64,2048]{2,1,0:T(8,128)(2,1)} %all-to-all-done.5, s32[1024]{0:T(1024)S(1)} %pad_clamp_fusion), kind=kCustom, calls=%fused_computation.3.clone | custom fusion | bytes 8388672 | tf_op jit(solution)/shard_map/jit(_take)/gather | solution.py:123
  118.6 3.0 %fusion.9 = bf16[16,2,2048]{2,1,0:T(2,128)(2,1)S(1)} fusion(bf16[16,64,2048]{2,1,0:T(8,128)(2,1)} %gather_fusion.9, pred[16]{0:T(512)(128)(4,1)S(1)} %get-tuple-element.16, bf16[16,2,2048]{2,1,0:T(2,128)(2,1)S(1)} %copy-done.10, bf16[16,2,64]{2,1,0:T(2,128)(2,1)S(1)} %reduce_sum.51), kind=kOutput, calls=%fused_computation.18 | convolution fusion | flops 10682368 | bytes 4460560 | tf_op jit(solution)/shard_map/gxj,gjv->gxv/dot_general | solution.py:128
  121.6 0.9 fusion.42
  122.6 12.1 %all-to-all-done.1 = bf16[2,4,3,128,256]{4,3,2,0,1:T(8,128)(2,1)} async-done(((bf16[2,4,3,128,256]{4,3,2,0,1:T(8,128)(2,1)}), bf16[2,4,3,128,256]{4,3,2,0,1:T(8,128)(2,1)}, u32[]{:S(2)}, u32[]{:S(2)}) %all-to-all-start.1) | async-done | bytes 1572896 | tf_op jit(solution)/shard_map/all_to_all | solution.py:136
  134.6 1.7 %copy.108 = bf16[2,4,3,128,256]{4,3,2,1,0:T(8,128)(2,1)S(1)} copy(bf16[2,4,3,128,256]{4,3,2,0,1:T(8,128)(2,1)} %all-to-all-done.1) | data formatting | bytes 3145728 | tf_op jit(solution)/shard_map/all_to_all | solution.py:136
  136.3 0.4 copy-done.2
  136.7 2.1 %pad_maximum_fusion = bf16[2,28,128,256]{3,2,1,0:T(8,128)(2,1)} fusion(bf16[2,12,128,256]{3,2,1,0:T(8,128)(2,1)S(1)} %bitcast.54, bf16[2,16,128,256]{3,2,1,0:T(8,128)(2,1)S(1)} %copy-done.2), kind=kLoop, calls=%fused_computation.16 | loop fusion | flops 1835008 | bytes 7340032 | tf_op jit(solution)/shard_map/concatenate | solution.py:137
  138.8 4.2 %gather_fusion.2 = bf16[16,2,128,256]{3,2,1,0:T(8,128)(2,1)} fusion(bf16[2,28,128,256]{3,2,1,0:T(8,128)(2,1)} %pad_maximum_fusion, s32[1024]{0:T(1024)} %pad_clamp_fusion.4), kind=kCustom, calls=%fused_computation.6 | custom fusion | bytes 4194368 | tf_op jit(solution)/shard_map/jit(_take)/gather | solution.py:141
  143.0 1.9 %select_bitcast_fusion = bf16[2,16,128,256]{3,2,0,1:T(8,128)(2,1)S(1)} fusion(bf16[16,2,128,256]{3,2,1,0:T(8,128)(2,1)} %gather_fusion.2, pred[16]{0:T(512)(128)(4,1)S(1)} %copy-done.8), kind=kLoop, calls=%fused_computation.22 | loop fusion | flops 1048576 | bytes 4194320 | tf_op jit(solution)/shard_map/jit(_take)/select_n | solution.py:141
  144.8 1.5 fusion.40
  146.3 1.5 copy.125
  147.8 1.6 %copy.111 = bf16[1,16,128,256]{2,3,1,0:T(8,128)(2,1)S(1)} copy(bf16[1,16,128,256]{3,2,0,1:T(8,128)(2,1)} %get-tuple-element.23) | data formatting | bytes 2097152 | tf_op jit(solution)/shard_map/slice | solution.py:142
  149.4 1.2 fusion.41
  150.6 0.8 reduce_max.32
  151.4 0.3 fusion.24
  151.7 0.9 divide_convert_fusion
  152.6 1.7 %copy.109 = bf16[1,16,128,256]{2,3,1,0:T(8,128)(2,1)S(1)} copy(bf16[1,16,128,256]{3,2,0,1:T(8,128)(2,1)} %get-tuple-element.24) | data formatting | bytes 2097152 | tf_op jit(solution)/shard_map/slice | solution.py:142
  154.3 0.6 convolution_bitcast_fusion.1
  154.9 0.2 fusion.19
  155.1 0.7 reshape.373
  (57 shorter events, 1.4 us)
Async XLA Ops:
  0.6 67.9 %copy-start = (bf16[2,128,16,256]{3,2,1,0:T(8,128)(2,1)S(1)}, bf16[2,128,16,256]{3,2,1,0:T(8,128)(2,1)}, u32[]{:S(2)}) copy-start(bf16[2,128,16,256]{3,2,1,0:T(8,128)(2,1)} %param.22) | copy-start | bytes 6291460
  4.2 12.9 %all-to-all-start.3 = ((s32[4,1,1]{2,1,0:T(1,128)}), s32[4,1,1]{2,1,0:T(1,128)S(1)}, u32[]{:S(2)}, u32[]{:S(2)}) async-start(s32[4,1,1]{2,1,0:T(1,128)} %copy.112), calls=%async_computation.3 | async-start | bytes 4096 | tf_op jit(solution)/shard_map/all_to_all | solution.py:99
  17.1 10.6 %all-to-all-start = ((s32[4,1,3]{2,1,0:T(1,128)}), s32[4,1,3]{2,1,0:T(1,128)S(1)}, u32[]{:S(2)}, u32[]{:S(2)}) async-start(s32[4,1,3]{2,1,0:T(1,128)} %bitcast), calls=%async_computation | async-start | bytes 4096 | tf_op jit(solution)/shard_map/all_to_all | solution.py:100
  27.6 9.5 %all-to-all-start.2 = ((s32[4,1,3]{2,1,0:T(1,128)}), s32[4,1,3]{2,1,0:T(1,128)S(1)}, u32[]{:S(2)}, u32[]{:S(2)}) async-start(s32[4,1,3]{2,1,0:T(1,128)} %bitcast.10), calls=%async_computation.2 | async-start | bytes 4096 | tf_op jit(solution)/shard_map/all_to_all | solution.py:103
  34.6 6.1 %copy-start.5 = (s32[16,8]{0,1:T(8,128)S(1)}, s32[16,8]{0,1:T(8,128)}, u32[]{:S(2)}) copy-start(s32[16,8]{0,1:T(8,128)} %param.23) | copy-start | bytes 1540
  37.1 27.1 %all-to-all-start.4 = ((bf16[4,64,2048]{2,1,0:T(8,128)(2,1)}), bf16[4,64,2048]{2,1,0:T(8,128)(2,1)S(1)}, u32[]{:S(2)}, u32[]{:S(2)}) async-start(bf16[4,64,2048]{2,1,0:T(8,128)(2,1)} %get-tuple-element.25), calls=%async_computation.4 | async-start | bytes 2097152 | tf_op jit(solution)/shard_map/all_to_all | solution.py:115
  64.2 29.5 %all-to-all-start.5 = ((bf16[4,64,2048]{2,1,0:T(8,128)(2,1)}), bf16[4,64,2048]{2,1,0:T(8,128)(2,1)}, u32[]{:S(2)}, u32[]{:S(2)}) async-start(bf16[4,64,2048]{2,1,0:T(8,128)(2,1)} %get-tuple-element.26), calls=%async_computation.5 | async-start | bytes 2097152 | tf_op jit(solution)/shard_map/all_to_all | solution.py:118
  76.7 3.5 %copy-start.4 = (bf16[16,2,2,256]{3,2,1,0:T(2,128)(2,1)S(1)}, bf16[16,2,2,256]{3,2,1,0:T(2,128)(2,1)}, u32[]{:S(2)}) copy-start(bf16[16,2,2,256]{3,2,1,0:T(2,128)(2,1)} %param.17) | copy-start | bytes 98308
  83.8 17.4 %copy-start.7 = (s32[16]{0:T(128)S(1)}, s32[16]{0:T(128)}, u32[]{:S(2)}) copy-start(s32[16]{0:T(128)} %param.25) | copy-start | bytes 196
  83.8 18.6 %copy-start.1 = (s32[16]{0:T(128)S(1)}, s32[16]{0:T(128)}, u32[]{:S(2)}) copy-start(s32[16]{0:T(128)} %param.24) | copy-start | bytes 196
  93.8 40.9 %all-to-all-start.1 = ((bf16[2,4,3,128,256]{4,3,2,0,1:T(8,128)(2,1)}), bf16[2,4,3,128,256]{4,3,2,0,1:T(8,128)(2,1)}, u32[]{:S(2)}, u32[]{:S(2)}) async-start(bf16[2,4,3,128,256]{4,3,2,0,1:T(8,128)(2,1)} %copy_select_fusion), calls=%async_computation.1 | async-start | bytes 3145728 | tf_op jit(solution)/shard_map/all_to_all | solution.py:136
  103.1 2.7 %copy-start.9 = (bf16[16,2,2048]{2,1,0:T(2,128)(2,1)S(1)}, bf16[16,2,2048]{2,1,0:T(2,128)(2,1)}, u32[]{:S(2)}) copy-start(bf16[16,2,2048]{2,1,0:T(2,128)(2,1)} %param.15) | copy-start | bytes 393220
  114.6 4.0 %copy-start.10 = (bf16[16,2,2048]{2,1,0:T(2,128)(2,1)S(1)}, bf16[16,2,2048]{2,1,0:T(2,128)(2,1)}, u32[]{:S(2)}) copy-start(bf16[16,2,2048]{2,1,0:T(2,128)(2,1)} %param.16) | copy-start | bytes 393220
  118.6 3.1 %copy-start.6 = (bf16[16,2,2,128]{3,2,1,0:T(2,128)(2,1)S(1)}, bf16[16,2,2,128]{3,2,1,0:T(2,128)(2,1)}, u32[]{:S(2)}) copy-start(bf16[16,2,2,128]{3,2,1,0:T(2,128)(2,1)} %reshape.371) | copy-start | bytes 49156
  118.6 3.1 %copy-start.11 = (pred[2,2]{1,0:T(4,128)(4,1)S(1)}, pred[2,2]{1,0:T(4,128)(4,1)}, u32[]{:S(2)}) copy-start(pred[2,2]{1,0:T(4,128)(4,1)} %iota_compare_fusion.5) | copy-start | bytes 16
  134.6 2.1 %copy-start.2 = (bf16[2,16,128,256]{3,2,1,0:T(8,128)(2,1)S(1)}, bf16[2,16,128,256]{3,2,1,0:T(8,128)(2,1)}, u32[]{:S(2)}) copy-start(bf16[2,16,128,256]{3,2,1,0:T(8,128)(2,1)} %bitcast_select_fusion) | copy-start | bytes 6291460
  138.8 4.2 %copy-start.8 = (pred[16]{0:T(512)(128)(4,1)S(1)}, pred[16]{0:T(512)(128)(4,1)}, u32[]{:S(2)}) copy-start(pred[16]{0:T(512)(128)(4,1)} %get-tuple-element.19) | copy-start | bytes 52
  152.6 1.7 %copy-start.3 = (bf16[16,2,2,8,130]{4,3,1,2,0:T(8,128)(2,1)S(1)}, bf16[16,2,2,8,130]{4,3,1,2,0:T(8,128)(2,1)}, u32[]{:S(2)}) copy-start(bf16[16,2,2,8,130]{4,3,1,2,0:T(8,128)(2,1)} %divide_convert_fusion) | copy-start | bytes 399364
